TPU v7x, 32 devices: a whole 2x2x4 slice. The times are simulated.
32 devices in a mesh: gx: 4 (over z), gy: 8 (over y, x, core).
Axes of the slice: x: 2, y: 2, z: 4, core: 2. Of those that a mesh axis runs over, the one named last changes fastest.
Arguments:
- velocity: float32 [3, 64, 256, 512], P(None, None, 'gy', 'gx'), may hold values from -6 to 6
- pressure: float32 [64, 256, 512], P(None, 'gy', 'gx'), may hold values from -6 to 6
- memory: float32 [64, 256, 512], P(None, 'gy', 'gx'), may hold values from -4 to 4
- buoyancy: float32 [64, 256, 512], P(None, 'gy', 'gx'), may hold values from 0.1 to 0.4
- modulus: float32 [64, 256, 512], P(None, 'gy', 'gx'), may hold values from 0.1 to 0.4
- relax: float32 [64, 256, 512], P(None, 'gy', 'gx'), may hold values from 0.05 to 0.5
- strength: float32 [64, 256, 512], P(None, 'gy', 'gx'), may hold values from 0.2 to 1
- spectra: float32 [2048, 256], P(('gx', 'gy')), may hold values from -6 to 6
- patch_cell: int32 [2048], P(('gx', 'gy')), may hold values from 0 to 262143
- rupture_patches: int32 [32, 64], replicated, may hold values from -1 to 2047, as said below
- slip_weights: bfloat16 [32, 64, 512], P('gx', 'gy'), may hold values from -1 to 1
Outputs:
- velocity_out: float32 [3, 64, 256, 512], P(None, None, 'gy', 'gx')
- pressure_out: float32 [64, 256, 512], P(None, 'gy', 'gx')
- memory_out: float32 [64, 256, 512], P(None, 'gy', 'gx')
- spectra_out: float32 [2048, 256], P(('gx', 'gy'))
- slip_response: float32 [32, 512, 256], P('gx', 'gy')
Inputs may be any that keep to these rules, and one draw needn't show every extreme that they name: `patch_cell`: the cell of a patch is a flat index (z * 32 + y) * 128 + x within its brick. `rupture_patches`: each patch is listed in at most one slot. Slot (r, s) belongs to the owner at index r // 8 of gx and s // 8 of gy; of the 64 patches of one block, at most 2 are listed in the slots of any one owner, and some pairs of block and owner reach 2.
All inputs are finite; a program needn't handle non-finite values.
Results may differ from a plain program's by a relative error of at most 0.0029.
Values may be sent and summed in bfloat16 or wider, within the bound.
A program may use at most 128 MiB of HBM per device.

v0:
```python
import functools

import jax
import jax.numpy as jnp
from jax import lax
from jax.experimental import pallas as pl
from jax.experimental.pallas import tpu as pltpu
from jax.sharding import PartitionSpec as P

STEPS = 4
CAP = 2
BATCH = 4


def phase_row(freqs, step):
    angle = jnp.pi * (jnp.arange(freqs, dtype=jnp.float32) + 0.5) / freqs * step
    return jnp.concatenate([jnp.cos(angle), -jnp.sin(angle)])


Y_ROWS = [4] + [3] * (STEPS - 1) + [1]
X_PACKS = [3] + [2] * (STEPS - 1) + [1]


def step_kernel(dims, *refs):
    nz, ny, nx, chunks, zc, per_dev, ngx, ngy = dims
    refs = list(refs)
    take = lambda count: [refs.pop(0) for _ in range(count)]
    vel_in, p_in, m_in, b_in, mod_in, rel_in, str_in, spectra, cell, cell_col, phase = take(11)
    vel_out, p_out, m_out, spectra_out = take(4)
    vx, vy, vz, p, m, b, mod, rel, stg = take(9)
    ysend, yrecv = (take(STEPS + 1), take(STEPS + 1))
    xsend, xrecv = (take(STEPS + 1), take(STEPS + 1))
    vxh, bxh, hx, vyh, rows_got, samples = take(6)
    in_sem, out_sem, send_sem, recv_sem = take(4)

    gx, gy = (lax.axis_index("gx"), lax.axis_index("gy"))
    has = [gy > 0, gy < ngy - 1, gx > 0, gx < ngx - 1]
    peer = [{"gy": gy - 1}, {"gy": gy + 1}, {"gx": gx - 1}, {"gx": gx + 1}]

    loads = [
        pltpu.make_async_copy(src, dst, in_sem.at[i])
        for i, (src, dst) in enumerate(
            [
                (p_in, p.at[pl.ds(1, nz)]),
                (b_in, b.at[pl.ds(0, nz)]),
                (vel_in.at[0], vx),
                (vel_in.at[1], vy),
                (vel_in.at[2], vz.at[pl.ds(1, nz)]),
                (rel_in, rel),
                (m_in, m),
                (str_in, stg),
                (mod_in, mod),
            ]
        )
    ]
    for load in loads:
        load.start()

    barrier = pltpu.get_barrier_semaphore()
    for side in range(4):

        @pl.when(has[side])
        def _():
            pl.semaphore_signal(
                barrier, inc=1, device_id=peer[side], device_id_type=pl.DeviceIdType.MESH
            )

    plane = jnp.zeros((ny, nx), jnp.float32)
    p[0] = plane
    p[nz + 1] = plane
    p[nz + 2] = plane
    vz[0] = plane
    vz[nz + 1] = plane
    b[nz] = plane
    for side in range(4):

        @pl.when(jnp.logical_not(has[side]))
        def _():
            for r in range(STEPS + 1):
                if side < 2:
                    yrecv[r][side] = jnp.zeros(yrecv[r].shape[1:], jnp.float32)
                else:
                    xrecv[r][side - 2] = jnp.zeros(xrecv[r].shape[1:], jnp.float32)

    def copy_to(r, c, side):
        slot = side % 2
        if side < 2:
            src, dst = (ysend[r].at[slot, c], yrecv[r].at[1 - slot, c])
        else:
            src, dst = (xsend[r].at[c], xrecv[r].at[1 - slot, c])
        return pltpu.make_async_remote_copy(
            src_ref=src,
            dst_ref=dst,
            send_sem=send_sem.at[r, c, side],
            recv_sem=recv_sem.at[r, c, side - side % 2 + 1 - slot],
            device_id=peer[side],
            device_id_type=pl.DeviceIdType.MESH,
        )

    def copy_from(r, c, side):
        slot = side % 2
        if side < 2:
            src, dst = (ysend[r].at[slot, c], yrecv[r].at[slot, c])
        else:
            src, dst = (xsend[r].at[c], xrecv[r].at[slot, c])
        return pltpu.make_async_remote_copy(
            src_ref=src,
            dst_ref=dst,
            send_sem=send_sem.at[r, c, side],
            recv_sem=recv_sem.at[r, c, side],
            device_id=peer[side],
            device_id_type=pl.DeviceIdType.MESH,
        )

    def send(r, c):
        for side in range(4):

            @pl.when(has[side])
            def _():
                copy_to(r, c, side).start()

    def receive(r, c):
        for side in range(4):

            @pl.when(has[side])
            def _():
                copy_from(r, c, side).wait_recv()

    lane = lax.broadcasted_iota(jnp.int32, (ny, nx), 1)
    row = lax.broadcasted_iota(jnp.int32, (ny, nx), 0)
    quad, lane4 = (lane // 4, lane % 4)
    last_lane, first_lane = (lane == nx - 1, lane == 0)
    last_row, first_row = (row == ny - 1, row == 0)

    def pack(total, slab, zl):
        return jnp.where(quad == zl, pltpu.roll(slab, 4 * zl + 2, 1), total)

    def d_x(slab, halo, zl):
        ends = pltpu.roll(halo, nx - 2 - 4 * zl, 1)
        after = jnp.where(last_lane, ends, pltpu.roll(slab, nx - 1, 1))
        before = jnp.where(first_lane, ends, pltpu.roll(slab, 1, 1))
        return after - before

    def d_y(slab, south, north):
        after = jnp.where(last_row, north, pltpu.roll(slab, ny - 1, 0))
        before = jnp.where(first_row, south, pltpu.roll(slab, 1, 0))
        return after - before

    for load in loads[:4]:
        load.wait()
    for c in range(chunks):

        def edges(i, totals):
            pt, vt, bt = totals
            for j in range(BATCH):
                zl = i * BATCH + j
                z = c * zc + zl
                ps, vs, ws, bs = (p[z + 1], vx[z], vy[z], b[z])
                pt, vt, bt = (pack(pt, ps, zl), pack(vt, vs, zl), pack(bt, bs, zl))
                at = pl.ds(zl, 1)
                ysend[0][0, c, 0, at, :] = ps[0:1]
                ysend[0][0, c, 1, at, :] = ps[1:2]
                ysend[0][0, c, 2, at, :] = ws[0:1]
                ysend[0][0, c, 3, at, :] = bs[0:1]
                ysend[0][1, c, 0, at, :] = ps[ny - 2 : ny - 1]
                ysend[0][1, c, 1, at, :] = ps[ny - 1 : ny]
                ysend[0][1, c, 2, at, :] = ws[ny - 1 : ny]
                ysend[0][1, c, 3, at, :] = bs[ny - 1 : ny]
            return pt, vt, bt

        totals = lax.fori_loop(0, zc // BATCH, edges, (plane, plane, plane))
        for i, total in enumerate(totals):
            xsend[0][c, i] = total
        if c == 0:
            pl.semaphore_wait(barrier, sum(side.astype(jnp.int32) for side in has))
        send(0, c)
    for load in loads[4:]:
        load.wait()

    def halos(r, c):
        def joined(i):
            return jnp.where(lane4 < 2, xrecv[r][0, c, i], xrecv[r][1, c, i])

        def swapped(halo):
            return jnp.where(lane4 == 1, pltpu.roll(halo, nx - 1, 1), pltpu.roll(halo, 1, 1))

        outer, own = (joined(0), xsend[r][c, 0])
        if r == 0:
            vh, bh = (joined(1), joined(2))
            bxh[c] = bh
            vyh[0, c] = yrecv[0][0, c, 2]
            vyh[1, c] = yrecv[0][1, c, 2]
        else:
            vh, bh = (vxh[c], bxh[c])
        slope = jnp.where(
            lane4 == 1,
            pltpu.roll(own, nx - 1, 1) - pltpu.roll(outer, 1, 1),
            pltpu.roll(outer, nx - 1, 1) - pltpu.roll(own, 1, 1),
        )
        vh = vh - bh * slope
        vxh[c] = vh
        hx[0, c] = swapped(outer)
        hx[1, c] = swapped(vh)
        vyh[0, c] = vyh[0, c] - yrecv[0][0, c, 3] * (ysend[r][0, c, 0] - yrecv[r][0, c, 0])
        vyh[1, c] = vyh[1, c] - yrecv[0][1, c, 3] * (yrecv[r][1, c, 1] - ysend[r][1, c, 1])

    def sweep(r, c):
        last = r == STEPS - 1
        n = r + 1

        def body(i, totals):
            pt, wt = totals
            base = i * BATCH
            z0 = c * zc + base
            ps = [p[z0 + 1 + j] for j in range(BATCH + 2)]
            bs = [b[z0 + j] for j in range(BATCH + 1)]
            zs = [vz[z0], vz[z0 + 1]]
            vs, ws, new_p = ([], [], [])
            for j in range(BATCH):
                zl = base + j
                at = pl.ds(zl, 1)
                zs.append(vz[z0 + j + 2] - bs[j + 1] * (ps[j + 2] - ps[j]))
                vs.append(vx[z0 + j] - bs[j] * d_x(ps[j], hx[0, c], zl))
                south, north = (yrecv[r][0, c, 1, at, :], yrecv[r][1, c, 0, at, :])
                ws.append(vy[z0 + j] - bs[j] * d_y(ps[j], south, north))
            for j in range(BATCH):
                zl = base + j
                at = pl.ds(zl, 1)
                spread = d_x(vs[j], hx[1, c], zl) + d_y(ws[j], vyh[0, c, at, :], vyh[1, c, at, :])
                spread = spread + (zs[j + 2] - zs[j])
                mem = m[z0 + j]
                mem = mem - rel[z0 + j] * (mem + stg[z0 + j] * spread)
                m[z0 + j] = mem
                new_p.append(ps[j] - mod[z0 + j] * (spread + mem))
            for j in range(BATCH):
                zl = base + j
                at = pl.ds(zl, 1)
                vz[z0 + j + 2] = zs[j + 2]
                vx[z0 + j] = vs[j]
                vy[z0 + j] = ws[j]
                p[z0 + j + 1] = new_p[j]
                wt = pack(wt, ws[j], zl)
                ysend[n][0, c, 0 if last else 2, at, :] = vs[j][0:1]
                ysend[n][1, c, 0 if last else 2, at, :] = vs[j][ny - 1 : ny]
                if not last:
                    pt = pack(pt, new_p[j], zl)
                    ysend[n][0, c, 0, at, :] = new_p[j][0:1]
                    ysend[n][0, c, 1, at, :] = new_p[j][1:2]
                    ysend[n][1, c, 0, at, :] = new_p[j][ny - 2 : ny - 1]
                    ysend[n][1, c, 1, at, :] = new_p[j][ny - 1 : ny]
            return pt, wt

        pt, wt = lax.fori_loop(0, zc // BATCH, body, (plane, plane))
        if last:
            xsend[n][c, 0] = wt
        else:
            xsend[n][c, 0] = pt
            xsend[n][c, 1] = wt

    cells = cell_col[...]
    cell_z, cell_y, cell_x = (cells // (ny * nx), (cells // nx) % ny, cells % nx)
    patch_lane = lax.broadcasted_iota(jnp.int32, (per_dev, nx), 1)

    def masked(keep, values):
        return jnp.where(keep, values, 0.0)

    def sample_own(n):
        def body(i, carry):
            at = cell[i]
            z, y = (at // (ny * nx), (at // nx) % ny)
            out = pl.ds(i, 1)
            rows_got[0, out, :] = vx[z, pl.ds(jnp.minimum(y + 1, ny - 1), 1), :]
            rows_got[1, out, :] = vx[z, pl.ds(jnp.maximum(y - 1, 0), 1), :]
            rows_got[2, out, :] = vy[z, pl.ds(y, 1), :]
            return carry

        lax.fori_loop(0, per_dev, body, 0, unroll=8)
        along = masked(cell_y < ny - 1, rows_got[0]) - masked(cell_y > 0, rows_got[1])
        across = rows_got[2]
        total = masked(patch_lane == cell_x, along)
        total = total + masked(patch_lane == cell_x + 1, across)
        samples[n - 1] = total - masked(patch_lane == cell_x - 1, across)

    def sample_halo(n):
        which_row, which_pack = (Y_ROWS[n] - 1, X_PACKS[n] - 1)

        def body(i, carry):
            at = cell[i]
            z, y = (at // (ny * nx), (at // nx) % ny)
            c, zl = (z // zc, z % zc)
            out = pl.ds(i, 1)
            rows_got[0, out, :] = yrecv[n][0, c, which_row, pl.ds(zl, 1), :]
            rows_got[1, out, :] = yrecv[n][1, c, which_row, pl.ds(zl, 1), :]
            rows_got[2, out, :] = xrecv[n][0, c, which_pack, pl.ds(y, 1), :]
            rows_got[3, out, :] = xrecv[n][1, c, which_pack, pl.ds(y, 1), :]
            return carry

        lax.fori_loop(0, per_dev, body, 0, unroll=8)
        start = 4 * (cell_z % zc)
        here = patch_lane == cell_x
        total = samples[n - 1]
        total = total + masked(here & (cell_y == ny - 1), rows_got[1])
        total = total - masked(here & (cell_y == 0), rows_got[0])
        total = total + masked((patch_lane == start + 2) & (cell_x == nx - 1), rows_got[3])
        total = total - masked((patch_lane == start + 1) & (cell_x == 0), rows_got[2])
        value = jnp.sum(total, axis=1, keepdims=True)
        spectra_out[...] = spectra_out[...] + value * phase[n - 1 : n, :]

    spectra_out[...] = spectra[...]
    stores = []
    for r in range(STEPS):
        vz[1] = vz[1] - b[0] * (p[2] - p[0])
        for c in range(chunks):
            receive(r, c)
            halos(r, c)
            sweep(r, c)
            send(r + 1, c)
            if r == STEPS - 1:
                at = pl.ds(c * zc, zc)
                pairs = [
                    (vx.at[at], vel_out.at[0, at]),
                    (vy.at[at], vel_out.at[1, at]),
                    (vz.at[pl.ds(1 + c * zc, zc)], vel_out.at[2, at]),
                    (p.at[pl.ds(1 + c * zc, zc)], p_out.at[at]),
                    (m.at[at], m_out.at[at]),
                ]
                for i, (src, dst) in enumerate(pairs):
                    store = pltpu.make_async_copy(src, dst, out_sem.at[c, i])
                    store.start()
                    stores.append(store)
        sample_own(r + 1)
        if r > 0:
            sample_halo(r)
    for c in range(chunks):
        receive(STEPS, c)
    sample_halo(STEPS)
    for r in range(STEPS + 1):
        for c in range(chunks):
            for side in range(4):

                @pl.when(has[side])
                def _():
                    copy_to(r, c, side).wait_send()

    for store in stores:
        store.wait()


def advance(velocity, pressure, memory, buoyancy, modulus, relax, strength, spectra, patch_cell):
    nz, ny, nx = pressure.shape
    per_dev, width = spectra.shape
    zc = nx // 4
    chunks = nz // zc
    dims = (nz, ny, nx, chunks, zc, per_dev, lax.axis_size("gx"), lax.axis_size("gy"))
    phase = jnp.stack([phase_row(width // 2, n + 1) for n in range(STEPS)])
    f32 = jnp.float32
    field = lambda planes: pltpu.VMEM((planes, ny, nx), f32)
    rounds = range(STEPS + 1)
    any_spec = pl.BlockSpec(memory_space=pl.ANY)
    vmem_spec = pl.BlockSpec(memory_space=pltpu.VMEM)
    return pl.pallas_call(
        functools.partial(step_kernel, dims),
        out_shape=[
            jax.ShapeDtypeStruct(velocity.shape, f32),
            jax.ShapeDtypeStruct(pressure.shape, f32),
            jax.ShapeDtypeStruct(memory.shape, f32),
            jax.ShapeDtypeStruct(spectra.shape, f32),
        ],
        in_specs=[any_spec] * 7
        + [vmem_spec, pl.BlockSpec(memory_space=pltpu.SMEM), vmem_spec, vmem_spec],
        out_specs=[any_spec] * 3 + [vmem_spec],
        scratch_shapes=[field(nz), field(nz), field(nz + 2), field(nz + 3), field(nz)]
        + [field(nz + 1), field(nz), field(nz), field(nz)]
        + [pltpu.VMEM((2, chunks, Y_ROWS[r], zc, nx), f32) for r in rounds]
        + [pltpu.VMEM((2, chunks, Y_ROWS[r], zc, nx), f32) for r in rounds]
        + [pltpu.VMEM((chunks, X_PACKS[r], ny, nx), f32) for r in rounds]
        + [pltpu.VMEM((2, chunks, X_PACKS[r], ny, nx), f32) for r in rounds]
        + [
            pltpu.VMEM((chunks, ny, nx), f32),
            pltpu.VMEM((chunks, ny, nx), f32),
            pltpu.VMEM((2, chunks, ny, nx), f32),
            pltpu.VMEM((2, chunks, zc, nx), f32),
            pltpu.VMEM((4, per_dev, nx), f32),
            pltpu.VMEM((STEPS, per_dev, nx), f32),
            pltpu.SemaphoreType.DMA((9,)),
            pltpu.SemaphoreType.DMA((chunks, 5)),
            pltpu.SemaphoreType.DMA((STEPS + 1, chunks, 4)),
            pltpu.SemaphoreType.DMA((STEPS + 1, chunks, 4)),
        ],
        compiler_params=pltpu.CompilerParams(collective_id=0, has_side_effects=True),
    )(
        velocity,
        pressure,
        memory,
        buoyancy,
        modulus,
        relax,
        strength,
        spectra,
        patch_cell,
        patch_cell.reshape(-1, 1),
        phase,
    )


def per_device(
    velocity,
    pressure,
    memory,
    buoyancy,
    modulus,
    relax,
    strength,
    spectra,
    patch_cell,
    rupture_patches,
    slip_weights,
):
    velocity_out, pressure, memory, spectra = advance(
        velocity, pressure, memory, buoyancy, modulus, relax, strength, spectra, patch_cell
    )
    freqs = spectra.shape[1] // 2
    groups_x = lax.axis_size("gx")
    groups_y = lax.axis_size("gy")
    devices = groups_x * groups_y
    owner = lax.axis_index("gx") * groups_y + lax.axis_index("gy")
    per_dev = spectra.shape[0]
    rup_group, slot_dev, variations = slip_weights.shape
    slots = rupture_patches.shape[1]
    flat_ids = rupture_patches.reshape(-1)
    slot_index = jnp.arange(flat_ids.shape[0], dtype=jnp.int32)
    target = slot_index // slots // rup_group * groups_y + slot_index % slots // slot_dev
    own_ids = owner * per_dev + jnp.arange(per_dev, dtype=jnp.int32)
    matches = flat_ids[None, :] == own_ids[:, None]
    target_of = jnp.max(jnp.where(matches, target[None, :], -1), axis=1)
    counter = jnp.arange(per_dev, dtype=jnp.int32)
    before = counter[None, :] < counter[:, None]
    rank = jnp.sum(((target_of[None, :] == target_of[:, None]) & before).astype(jnp.int32), axis=1)
    bucket = jnp.where(target_of >= 0, target_of * CAP + rank, -1)
    placing = (jnp.arange(devices * CAP, dtype=jnp.int32)[:, None] == bucket[None, :]).astype(
        jnp.bfloat16
    )
    rounded = spectra.astype(jnp.bfloat16)
    outgoing = jnp.dot(placing, rounded, preferred_element_type=jnp.float32).astype(jnp.bfloat16)
    outgoing = outgoing.reshape(devices, CAP, 2 * freqs)
    incoming = lax.all_to_all(outgoing, ("gx", "gy"), split_axis=0, concat_axis=0, tiled=True)
    received = incoming.reshape(devices * CAP, 2 * freqs)
    local_ids = lax.dynamic_slice(
        rupture_patches,
        (lax.axis_index("gx") * rup_group, lax.axis_index("gy") * slot_dev),
        (rup_group, slot_dev),
    ).reshape(-1)
    source = local_ids // per_dev
    earlier_slot = (
        (local_ids[None, :] < local_ids[:, None])
        & (source[None, :] == source[:, None])
        & (local_ids[None, :] >= 0)
    )
    rank_in = jnp.sum(earlier_slot.astype(jnp.int32), axis=1)
    live = local_ids >= 0
    row = jnp.where(live, source * CAP + rank_in, 0)
    picked = jnp.take(received, row, axis=0)
    slot_spectra = jnp.where(live[:, None], picked, jnp.zeros_like(picked)).reshape(
        rup_group, slot_dev, 2 * freqs
    )
    swapped = lax.all_to_all(slip_weights, "gy", split_axis=2, concat_axis=1, tiled=True)
    slip = jnp.einsum(
        "rsv,rsf->rvf",
        swapped,
        lax.all_gather(slot_spectra, "gy", axis=1, tiled=True),
        preferred_element_type=jnp.float32,
    )
    return (velocity_out, pressure, memory, spectra, slip)


def solution(mesh):
    in_specs = (
        P(None, None, "gy", "gx"),
        P(None, "gy", "gx"),
        P(None, "gy", "gx"),
        P(None, "gy", "gx"),
        P(None, "gy", "gx"),
        P(None, "gy", "gx"),
        P(None, "gy", "gx"),
        P(("gx", "gy"), None),
        P(("gx", "gy")),
        P(),
        P("gx", "gy", None),
    )
    out_specs = (
        P(None, None, "gy", "gx"),
        P(None, "gy", "gx"),
        P(None, "gy", "gx"),
        P(("gx", "gy"), None),
        P("gx", "gy", None),
    )
    return jax.shard_map(
        per_device, mesh=mesh, in_specs=in_specs, out_specs=out_specs, check_vma=False
    )
```

profile of v0, /device:TPU:0, one launch (start us, length us, event | category | flops | bytes accessed | tf_op | source)
XLA Modules:
  0.0 82.1 jit_solution(17780366101891603162)
XLA Ops:
  0.6 1.6 %copy.29 = bf16[8,8,512]{1,0,2:T(8,128)(2,1)S(1)} copy(bf16[8,8,512]{2,1,0:T(8,128)(2,1)} %param.21) | data formatting | bytes 131072 | tf_op args[10]
  2.2 1.7 %reshape.272 = bf16[8,2,2048]{2,1,0:T(2,128)(2,1)} reshape(bf16[512,8,8]{2,1,0:T(8,128)(2,1)S(1)} %bitcast.30) | data formatting | bytes 131072
  3.9 5.2 %all-to-all-start.1 = ((bf16[8,2,2048]{2,1,0:T(2,128)(2,1)}), bf16[8,2,2048]{2,1,0:T(2,128)(2,1)S(1)}, u32[]{:S(2)}, u32[]{:S(2)}) async-start(bf16[8,2,2048]{2,1,0:T(2,128)(2,1)} %reshape.272), calls=%async_computation.1 | async-start | bytes 131072 | tf_op jit(solution)/shard_map/all_to_all | solution.py:466
  9.3 0.8 eq.62
  10.1 0.8 broadcast_compare_fusion
  10.9 0.1 reshape.260
  11.0 0.1 reshape.263
  11.1 1.4 %copy.28.refs_9_ = s32[64,1]{1,0:T(8,128)} copy(s32[64,1]{0,1:T(1,128)} %bitcast.35) | data formatting | bytes 512 | tf_op jit(solution)/shard_map/reshape | solution.py:401
  12.4 0.2 select_reduce_fusion
  12.7 0.2 convert_reduce_fusion
  12.9 0.2 convert_reduce_fusion.1
  13.0 0.1 reduce_sum.23
  13.2 0.6 pad_maximum_fusion.refs_10_
  13.8 37.5 %shard_map.146 = (f32[3,64,32,128]{3,2,1,0:T(8,128)}, f32[64,32,128]{2,1,0:T(8,128)}, f32[64,32,128]{2,1,0:T(8,128)}, f32[64,256]{1,0:T(8,128)}) custom-call(f32[3,64,32,128]{3,2,1,0:T(8,128)} %refs_0_.1, f32[64,32,128]{2,1,0:T(8,128)} %refs_1_.1, f32[64,32,128]{2,1,0:T(8,128)} %refs_2_.1, f32[64,32,128]{2,1,0:T(8,128)} %refs_3_.1, f32[64,32,128]{2,1,0:T(8,128)} %refs_4_.1, ...), custom_call_target="tpu_custom_call" | custom-call | tf_op jit(solution)/shard_map/pallas_call | solution.py:361
  51.3 1.0 %convolution_convert_fusion = bf16[64,256]{1,0:T(8,128)(2,1)S(1)} fusion(f32[64,256]{1,0:T(8,128)} %get-tuple-element.31, s32[64]{0:T(128)S(1)} %compare_select_fusion.3), kind=kOutput, calls=%fused_computation.2 | convolution fusion | flops 2134016 | bytes 98560 | tf_op jit(solution)/shard_map/dot_general | solution.py:444
  52.3 0.6 reshape.261
  52.9 0.0 all-to-all-done.1
  52.9 4.6 %all-to-all-start = ((bf16[32,2,256]{2,1,0:T(2,128)(2,1)}), bf16[32,2,256]{2,1,0:T(2,128)(2,1)S(1)}, u32[]{:S(2)}, u32[]{:S(2)}) async-start(bf16[32,2,256]{2,1,0:T(2,128)(2,1)} %reshape.261), calls=%async_computation | async-start | bytes 65536 | tf_op jit(solution)/shard_map/all_to_all | solution.py:446
  57.5 1.2 %reshape.273 = bf16[512,8,8]{2,1,0:T(8,128)(2,1)S(1)} reshape(bf16[8,2,2048]{2,1,0:T(2,128)(2,1)S(1)} %all-to-all-done.1) | data formatting | bytes 131072
  58.7 0.7 copy.31
  59.5 5.3 %all-to-all-done = bf16[32,2,256]{2,1,0:T(2,128)(2,1)S(1)} async-done(((bf16[32,2,256]{2,1,0:T(2,128)(2,1)}), bf16[32,2,256]{2,1,0:T(2,128)(2,1)S(1)}, u32[]{:S(2)}, u32[]{:S(2)}) %all-to-all-start) | async-done | bytes 32800 | tf_op jit(solution)/shard_map/all_to_all | solution.py:446
  64.8 0.7 gather_fusion
  65.5 0.1 fusion.1
  65.6 8.9 %all_gather.3 = bf16[8,64,256]{2,1,0:T(8,128)(2,1)S(1)} all-gather(bf16[8,8,256]{2,1,0:T(8,128)(2,1)S(1)} %fusion.1), channel_id=1, replica_groups=mesh['gx'=4,'gy'=8] {'gy'}, dimensions={1}, use_global_device_ids=true | all-gather | bytes 294912 | tf_op jit(solution)/shard_map/all_gather | solution.py:470
  74.5 1.1 %convolution_bitcast_fusion = f32[8,64,256]{2,1,0:T(8,128)} fusion(bf16[8,64,256]{2,1,0:T(8,128)(2,1)S(1)} %all_gather.3, bf16[8,8,8,64]{3,2,1,0:T(8,128)(2,1)S(1)} %copy.31), kind=kOutput, calls=%fused_computation.1 | convolution fusion | flops 16777216 | bytes 851968 | tf_op jit(solution)/shard_map/rsv,rsf->rvf/dot_general | solution.py:467
  75.5 0.0 copy-start.1
  75.6 0.0 copy-start
  75.6 4.0 %copy.40 = f32[3,64,32,128]{3,2,1,0:T(8,128)} copy(f32[3,64,32,128]{3,2,1,0:T(8,128)} %get-tuple-element.28) | data formatting | bytes 6291456
  79.6 0.0 copy-done.1
  79.6 0.0 copy-start.2
  79.6 1.0 %copy.41 = f32[64,32,128]{2,1,0:T(8,128)} copy(f32[64,32,128]{2,1,0:T(8,128)S(1)} %copy-done.1) | data formatting | bytes 2097152
  80.5 0.0 copy-done
  80.5 1.0 %copy.42 = f32[64,32,128]{2,1,0:T(8,128)} copy(f32[64,32,128]{2,1,0:T(8,128)S(1)} %copy-done) | data formatting | bytes 2097152
  81.5 0.0 copy-done.2
  81.5 0.6 copy.43
  (17 shorter events, 0.3 us)
Async XLA Ops:
  3.9 49.0 %all-to-all-start.1 = ((bf16[8,2,2048]{2,1,0:T(2,128)(2,1)}), bf16[8,2,2048]{2,1,0:T(2,128)(2,1)S(1)}, u32[]{:S(2)}, u32[]{:S(2)}) async-start(bf16[8,2,2048]{2,1,0:T(2,128)(2,1)} %reshape.272), calls=%async_computation.1 | async-start | bytes 131072 | tf_op jit(solution)/shard_map/all_to_all | solution.py:466
  52.9 11.8 %all-to-all-start = ((bf16[32,2,256]{2,1,0:T(2,128)(2,1)}), bf16[32,2,256]{2,1,0:T(2,128)(2,1)S(1)}, u32[]{:S(2)}, u32[]{:S(2)}) async-start(bf16[32,2,256]{2,1,0:T(2,128)(2,1)} %reshape.261), calls=%async_computation | async-start | bytes 65536 | tf_op jit(solution)/shard_map/all_to_all | solution.py:446
  75.5 4.0 %copy-start.1 = (f32[64,32,128]{2,1,0:T(8,128)S(1)}, f32[64,32,128]{2,1,0:T(8,128)}, u32[]{:S(2)}) copy-start(f32[64,32,128]{2,1,0:T(8,128)} %get-tuple-element.29) | copy-start | bytes 3145732
  75.6 5.0 %copy-start = (f32[64,32,128]{2,1,0:T(8,128)S(1)}, f32[64,32,128]{2,1,0:T(8,128)}, u32[]{:S(2)}) copy-start(f32[64,32,128]{2,1,0:T(8,128)} %get-tuple-element.30) | copy-start | bytes 3145732
  79.6 1.9 %copy-start.2 = (f32[64,256]{1,0:T(8,128)S(1)}, f32[64,256]{1,0:T(8,128)}, u32[]{:S(2)}) copy-start(f32[64,256]{1,0:T(8,128)} %get-tuple-element.31) | copy-start | bytes 196612
where the time goes:
time: 82.6 us; the launch traced here: 82.1 us
  Pallas kernels  37.5 us (45%)
  local copies, waits for them, and re-layouts  15.5 us (19%)
  starting transfers between devices  9.76 us (12%)
  blocking collectives  8.9 us (11%)
  waiting for transfers between devices  5.3 us (6%)
  other arithmetic  2.36 us (3%)
  matrix products  2.04 us (2%)
    pallas_call x1, Pallas kernels, advance(): pl.pallas_call(functools.partial(step_kernel, dims), out_shape=[jax.Shape...  37.5 us
    unnamed x13, local copies, waits for them, and re-layouts  11 us
    all_gather x1, blocking collectives, per_device(): lax.all_gather(slot_spectra, 'gy', axis=1, tiled=True)  8.9 us
    all_to_all x1, waiting for transfers between devices, per_device(): lax.all_to_all(outgoing, ('gx', 'gy'), split_axis=0, concat_axis=0, tiled...  5.29 us
    all_to_all x1, starting transfers between devices, per_device(): lax.all_to_all(slip_weights, 'gy', split_axis=2, concat_axis=1, tiled=True)  5.2 us
    all_to_all x1, starting transfers between devices, per_device(): lax.all_to_all(outgoing, ('gx', 'gy'), split_axis=0, concat_axis=0, tiled...  4.56 us
  transfers between devices with their start and end apart: 2, of which 1 were waited for; matrix products, arithmetic and copies ran while one was open for 10% of the time, Pallas kernels for 46%

commit v1 on v0

--- a/solution.py
+++ b/solution.py
@@ -2,6 +2,7 @@
 
 import jax
 import jax.numpy as jnp
+import numpy as np
 from jax import lax
 from jax.experimental import pallas as pl
 from jax.experimental.pallas import tpu as pltpu
@@ -12,9 +13,10 @@
 BATCH = 4
 
 
-def phase_row(freqs, step):
-    angle = jnp.pi * (jnp.arange(freqs, dtype=jnp.float32) + 0.5) / freqs * step
-    return jnp.concatenate([jnp.cos(angle), -jnp.sin(angle)])
+def phase_rows(freqs):
+    angle = np.pi * (np.arange(freqs) + 0.5) / freqs
+    rows = [np.concatenate([np.cos(angle * n), -np.sin(angle * n)]) for n in range(1, STEPS + 1)]
+    return jnp.asarray(np.stack(rows).astype(np.float32))
 
 
 Y_ROWS = [4] + [3] * (STEPS - 1) + [1]
@@ -25,13 +27,15 @@
     nz, ny, nx, chunks, zc, per_dev, ngx, ngy = dims
     refs = list(refs)
     take = lambda count: [refs.pop(0) for _ in range(count)]
-    vel_in, p_in, m_in, b_in, mod_in, rel_in, str_in, spectra, cell, cell_col, phase = take(11)
-    vel_out, p_out, m_out, spectra_out = take(4)
+    vel_in, p_in, m_in, b_in, mod_in, rel_in, str_in, spectra, cell, cell_row, phase = take(11)
+    listed, weights = take(2)
+    vel_out, p_out, m_out, spectra_out, weights_got, rows_out = take(6)
     vx, vy, vz, p, m, b, mod, rel, stg = take(9)
     ysend, yrecv = (take(STEPS + 1), take(STEPS + 1))
     xsend, xrecv = (take(STEPS + 1), take(STEPS + 1))
     vxh, bxh, hx, vyh, rows_got, samples = take(6)
-    in_sem, out_sem, send_sem, recv_sem = take(4)
+    placing, rows_send, rows_group = take(3)
+    in_sem, out_sem, send_sem, recv_sem, far_send, far_recv = take(6)
 
     gx, gy = (lax.axis_index("gx"), lax.axis_index("gy"))
     has = [gy > 0, gy < ngy - 1, gx > 0, gx < ngx - 1]
@@ -56,14 +60,14 @@
     for load in loads:
         load.start()
 
+    along_gx = [lax.rem(gx + k, ngx) for k in range(1, ngx)]
+    along_gy = [lax.rem(gy + k, ngy) for k in range(1, ngy)]
+    peers = [{"gx": other} for other in along_gx] + [{"gy": other} for other in along_gy]
     barrier = pltpu.get_barrier_semaphore()
-    for side in range(4):
-
-        @pl.when(has[side])
-        def _():
-            pl.semaphore_signal(
-                barrier, inc=1, device_id=peer[side], device_id_type=pl.DeviceIdType.MESH
-            )
+    for other in peers:
+        pl.semaphore_signal(
+            barrier, inc=1, device_id=other, device_id_type=pl.DeviceIdType.MESH
+        )
 
     plane = jnp.zeros((ny, nx), jnp.float32)
     p[0] = plane
@@ -172,10 +176,88 @@
         for i, total in enumerate(totals):
             xsend[0][c, i] = total
         if c == 0:
-            pl.semaphore_wait(barrier, sum(side.astype(jnp.int32) for side in has))
+            pl.semaphore_wait(barrier, len(peers))
         send(0, c)
     for load in loads[4:]:
         load.wait()
+
+    rup_group, slot_dev, variations = weights.shape
+    lanes = weights_got.shape[3]
+    group_rows = ngy * CAP
+    all_rows = ngx * group_rows
+
+    def weight_block(other):
+        block = other * (variations // ngy) // lanes
+        return weights.at[:, :, pl.ds(pl.multiple_of(block * lanes, lanes), lanes)]
+
+    def far(kind, k, src, dst):
+        axis, size = ("gx", ngx) if kind == 1 else ("gy", ngy)
+        return pltpu.make_async_remote_copy(
+            src_ref=src,
+            dst_ref=dst,
+            send_sem=far_send.at[kind, k],
+            recv_sem=far_recv.at[kind, k],
+            device_id={axis: lax.rem(lax.axis_index(axis) + k, size)},
+            device_id_type=pl.DeviceIdType.MESH,
+        )
+
+    def rows_of(ref, index, count):
+        return ref.at[pl.ds(pl.multiple_of(index * count, count), count)]
+
+    def weights_to(k):
+        return far(0, k, weight_block(lax.rem(gy + k, ngy)), weights_got.at[gy])
+
+    def weights_from(k):
+        return far(0, k, weight_block(gy), weights_got.at[lax.rem(gy + ngy - k, ngy)])
+
+    def first_to(k):
+        src = rows_of(rows_send, lax.rem(gx + k, ngx), group_rows)
+        return far(1, k, src, rows_of(rows_group, gx, group_rows))
+
+    def first_from(k):
+        src = rows_of(rows_send, gx, group_rows)
+        return far(1, k, src, rows_of(rows_group, lax.rem(gx + ngx - k, ngx), group_rows))
+
+    def second_to(k):
+        return far(2, k, rows_group, rows_of(rows_out, gy, all_rows))
+
+    def second_from(k):
+        return far(2, k, rows_group, rows_of(rows_out, lax.rem(gy + ngy - k, ngy), all_rows))
+
+    for k in range(1, ngy):
+        weights_to(k).start()
+    own_weights = pltpu.make_async_copy(weight_block(gy), weights_got.at[gy], far_send.at[0, 0])
+    own_weights.start()
+
+    square = (per_dev, per_dev)
+    eye = lax.broadcasted_iota(jnp.int32, square, 0) == lax.broadcasted_iota(jnp.int32, square, 1)
+
+    def to_row(column):
+        return jnp.sum(jnp.where(eye, column, 0.0), axis=0, keepdims=True)
+
+    def to_column(line):
+        return jnp.sum(jnp.where(eye, line, 0.0), axis=1, keepdims=True)
+
+    def fill_placing():
+        ruptures, slots = listed.shape
+        shape = (per_dev, slots)
+        own_ids = lax.broadcasted_iota(jnp.int32, shape, 0) + (gx * ngy + gy) * per_dev
+        slot_owner = lax.broadcasted_iota(jnp.int32, shape, 1) // slot_dev
+
+        def body(r, best):
+            owner = r // rup_group * ngy + slot_owner
+            return jnp.where(listed[pl.ds(r, 1), :] == own_ids, owner, best)
+
+        best = lax.fori_loop(0, ruptures, body, jnp.full(shape, -1, jnp.int32))
+        target = jnp.max(best.astype(jnp.float32), axis=1, keepdims=True)
+        before = lax.broadcasted_iota(jnp.int32, square, 1) < lax.broadcasted_iota(
+            jnp.int32, square, 0
+        )
+        same = (to_row(target) == target) & before
+        rank = jnp.sum(jnp.where(same, 1.0, 0.0), axis=1, keepdims=True)
+        bucket = to_row(jnp.where(target >= 0.0, target * CAP + rank, -1.0))
+        place = lax.broadcasted_iota(jnp.int32, placing.shape, 0).astype(jnp.float32)
+        placing[...] = jnp.where(place == bucket, 1.0, 0.0).astype(jnp.bfloat16)
 
     def halos(r, c):
         def joined(i):
@@ -257,7 +339,8 @@
             xsend[n][c, 0] = pt
             xsend[n][c, 1] = wt
 
-    cells = cell_col[...]
+    fill_placing()
+    cells = to_column(cell_row[...].astype(jnp.float32)).astype(jnp.int32)
     cell_z, cell_y, cell_x = (cells // (ny * nx), (cells // nx) % ny, cells % nx)
     patch_lane = lax.broadcasted_iota(jnp.int32, (per_dev, nx), 1)
 
@@ -334,6 +417,28 @@
     for c in range(chunks):
         receive(STEPS, c)
     sample_halo(STEPS)
+    rows_send[...] = jnp.dot(
+        placing[...], spectra_out[...].astype(jnp.bfloat16), preferred_element_type=jnp.float32
+    ).astype(jnp.bfloat16)
+    for k in range(1, ngx):
+        first_to(k).start()
+    at = pl.ds(pl.multiple_of(gx * group_rows, group_rows), group_rows)
+    rows_group[at, :] = rows_send[at, :]
+    for k in range(1, ngx):
+        first_from(k).wait_recv()
+    for k in range(1, ngy):
+        second_to(k).start()
+    at = pl.ds(pl.multiple_of(gy * all_rows, all_rows), all_rows)
+    rows_out[at, :] = rows_group[...]
+    own_weights.wait()
+    for k in range(1, ngy):
+        weights_from(k).wait_recv()
+        weights_to(k).wait_send()
+    for k in range(1, ngy):
+        second_from(k).wait_recv()
+        second_to(k).wait_send()
+    for k in range(1, ngx):
+        first_to(k).wait_send()
     for r in range(STEPS + 1):
         for c in range(chunks):
             for side in range(4):
@@ -346,13 +451,18 @@
         store.wait()
 
 
-def advance(velocity, pressure, memory, buoyancy, modulus, relax, strength, spectra, patch_cell):
+def advance(
+    velocity, pressure, memory, buoyancy, modulus, relax, strength, spectra, patch_cell, listed, weights
+):
     nz, ny, nx = pressure.shape
     per_dev, width = spectra.shape
     zc = nx // 4
     chunks = nz // zc
-    dims = (nz, ny, nx, chunks, zc, per_dev, lax.axis_size("gx"), lax.axis_size("gy"))
-    phase = jnp.stack([phase_row(width // 2, n + 1) for n in range(STEPS)])
+    ngx, ngy = (lax.axis_size("gx"), lax.axis_size("gy"))
+    dims = (nz, ny, nx, chunks, zc, per_dev, ngx, ngy)
+    rup_group, slot_dev, variations = weights.shape
+    lanes = max(variations // ngy, 128)
+    all_rows = ngx * ngy * CAP
     f32 = jnp.float32
     field = lambda planes: pltpu.VMEM((planes, ny, nx), f32)
     rounds = range(STEPS + 1)
@@ -365,10 +475,13 @@
             jax.ShapeDtypeStruct(pressure.shape, f32),
             jax.ShapeDtypeStruct(memory.shape, f32),
             jax.ShapeDtypeStruct(spectra.shape, f32),
+            jax.ShapeDtypeStruct((ngy, rup_group, slot_dev, lanes), jnp.bfloat16),
+            jax.ShapeDtypeStruct((ngy * all_rows, width), jnp.bfloat16),
         ],
         in_specs=[any_spec] * 7
-        + [vmem_spec, pl.BlockSpec(memory_space=pltpu.SMEM), vmem_spec, vmem_spec],
-        out_specs=[any_spec] * 3 + [vmem_spec],
+        + [vmem_spec, pl.BlockSpec(memory_space=pltpu.SMEM)]
+        + [vmem_spec] * 4,
+        out_specs=[any_spec] * 3 + [vmem_spec] * 3,
         scratch_shapes=[field(nz), field(nz), field(nz + 2), field(nz + 3), field(nz)]
         + [field(nz + 1), field(nz), field(nz), field(nz)]
         + [pltpu.VMEM((2, chunks, Y_ROWS[r], zc, nx), f32) for r in rounds]
@@ -382,10 +495,15 @@
             pltpu.VMEM((2, chunks, zc, nx), f32),
             pltpu.VMEM((4, per_dev, nx), f32),
             pltpu.VMEM((STEPS, per_dev, nx), f32),
+            pltpu.VMEM((all_rows, per_dev), jnp.bfloat16),
+            pltpu.VMEM((all_rows, width), jnp.bfloat16),
+            pltpu.VMEM((all_rows, width), jnp.bfloat16),
             pltpu.SemaphoreType.DMA((9,)),
             pltpu.SemaphoreType.DMA((chunks, 5)),
             pltpu.SemaphoreType.DMA((STEPS + 1, chunks, 4)),
             pltpu.SemaphoreType.DMA((STEPS + 1, chunks, 4)),
+            pltpu.SemaphoreType.DMA((3, max(ngx, ngy))),
+            pltpu.SemaphoreType.DMA((3, max(ngx, ngy))),
         ],
         compiler_params=pltpu.CompilerParams(collective_id=0, has_side_effects=True),
     )(
@@ -398,8 +516,10 @@
         strength,
         spectra,
         patch_cell,
-        patch_cell.reshape(-1, 1),
-        phase,
+        patch_cell.reshape(1, -1),
+        phase_rows(width // 2),
+        listed,
+        weights,
     )
 
 
@@ -416,60 +536,39 @@
     rupture_patches,
     slip_weights,
 ):
-    velocity_out, pressure, memory, spectra = advance(
-        velocity, pressure, memory, buoyancy, modulus, relax, strength, spectra, patch_cell
+    velocity_out, pressure, memory, spectra, weights, rows = advance(
+        velocity,
+        pressure,
+        memory,
+        buoyancy,
+        modulus,
+        relax,
+        strength,
+        spectra,
+        patch_cell,
+        rupture_patches,
+        slip_weights,
     )
-    freqs = spectra.shape[1] // 2
-    groups_x = lax.axis_size("gx")
-    groups_y = lax.axis_size("gy")
-    devices = groups_x * groups_y
-    owner = lax.axis_index("gx") * groups_y + lax.axis_index("gy")
+    groups_x, groups_y = (lax.axis_size("gx"), lax.axis_size("gy"))
     per_dev = spectra.shape[0]
     rup_group, slot_dev, variations = slip_weights.shape
-    slots = rupture_patches.shape[1]
-    flat_ids = rupture_patches.reshape(-1)
-    slot_index = jnp.arange(flat_ids.shape[0], dtype=jnp.int32)
-    target = slot_index // slots // rup_group * groups_y + slot_index % slots // slot_dev
-    own_ids = owner * per_dev + jnp.arange(per_dev, dtype=jnp.int32)
-    matches = flat_ids[None, :] == own_ids[:, None]
-    target_of = jnp.max(jnp.where(matches, target[None, :], -1), axis=1)
-    counter = jnp.arange(per_dev, dtype=jnp.int32)
-    before = counter[None, :] < counter[:, None]
-    rank = jnp.sum(((target_of[None, :] == target_of[:, None]) & before).astype(jnp.int32), axis=1)
-    bucket = jnp.where(target_of >= 0, target_of * CAP + rank, -1)
-    placing = (jnp.arange(devices * CAP, dtype=jnp.int32)[:, None] == bucket[None, :]).astype(
-        jnp.bfloat16
+    ids = lax.dynamic_slice_in_dim(
+        rupture_patches, lax.axis_index("gx") * rup_group, rup_group, axis=0
     )
-    rounded = spectra.astype(jnp.bfloat16)
-    outgoing = jnp.dot(placing, rounded, preferred_element_type=jnp.float32).astype(jnp.bfloat16)
-    outgoing = outgoing.reshape(devices, CAP, 2 * freqs)
-    incoming = lax.all_to_all(outgoing, ("gx", "gy"), split_axis=0, concat_axis=0, tiled=True)
-    received = incoming.reshape(devices * CAP, 2 * freqs)
-    local_ids = lax.dynamic_slice(
-        rupture_patches,
-        (lax.axis_index("gx") * rup_group, lax.axis_index("gy") * slot_dev),
-        (rup_group, slot_dev),
-    ).reshape(-1)
-    source = local_ids // per_dev
-    earlier_slot = (
-        (local_ids[None, :] < local_ids[:, None])
-        & (source[None, :] == source[:, None])
-        & (local_ids[None, :] >= 0)
-    )
-    rank_in = jnp.sum(earlier_slot.astype(jnp.int32), axis=1)
-    live = local_ids >= 0
-    row = jnp.where(live, source * CAP + rank_in, 0)
-    picked = jnp.take(received, row, axis=0)
-    slot_spectra = jnp.where(live[:, None], picked, jnp.zeros_like(picked)).reshape(
-        rup_group, slot_dev, 2 * freqs
-    )
-    swapped = lax.all_to_all(slip_weights, "gy", split_axis=2, concat_axis=1, tiled=True)
-    slip = jnp.einsum(
-        "rsv,rsf->rvf",
-        swapped,
-        lax.all_gather(slot_spectra, "gy", axis=1, tiled=True),
-        preferred_element_type=jnp.float32,
-    )
+    ids = ids.reshape(rup_group, groups_y, slot_dev).transpose(1, 0, 2).reshape(groups_y, -1)
+    source = ids // per_dev
+    earlier = (ids[:, None, :] < ids[:, :, None]) & (source[:, None, :] == source[:, :, None])
+    rank = jnp.sum((earlier & (ids[:, None, :] >= 0)).astype(jnp.int32), axis=2)
+    owner = jnp.arange(groups_y, dtype=jnp.int32)[:, None]
+    block = source % groups_y * groups_x + source // groups_y
+    row = jnp.where(ids >= 0, (block * groups_y + owner) * CAP + rank, -1)
+    chosen = (row[:, :, None] == jnp.arange(rows.shape[0], dtype=jnp.int32)).astype(jnp.bfloat16)
+    slot_spectra = jnp.einsum("gkq,qf->gkf", chosen, rows, preferred_element_type=jnp.float32)
+    slot_spectra = slot_spectra.astype(jnp.bfloat16).reshape(groups_y, rup_group, slot_dev, -1)
+    share = variations // groups_y
+    start = lax.axis_index("gy") * share % weights.shape[3]
+    own = lax.dynamic_slice_in_dim(weights, start, share, axis=3)
+    slip = jnp.einsum("grsv,grsf->rvf", own, slot_spectra, preferred_element_type=jnp.float32)
     return (velocity_out, pressure, memory, spectra, slip)
 
 

time: 82.6 us -> 59.5 us (0.72)
  Pallas kernels: 37.5 us -> 48.3 us
  starting transfers between devices: 9.76 us -> 0 us
  blocking collectives: 8.9 us -> 0 us
  local copies, waits for them, and re-layouts: 15.5 us -> 7.44 us
  waiting for transfers between devices: 5.3 us -> 0 us
  other arithmetic: 2.36 us -> 0.43 us
    pallas_call x1, Pallas kernels: 37.5 us -> 48.3 us  [advance(): pl.pallas_call(functools.partial(step_kernel, dims), out_shape=[jax.Shape...]
    all_to_all x2 -> x0, starting transfers between devices: 9.76 us -> none  [the longest x1 5.2 us: per_device(): lax.all_to_all(slip_weights, 'gy', split_axis=2, concat_axis=1, tiled=True)]
    all_gather x1 -> x0, blocking collectives: 8.9 us -> none  [per_device(): lax.all_gather(slot_spectra, 'gy', axis=1, tiled=True)]
    all_to_all x2 -> x0, waiting for transfers between devices: 5.3 us -> none  [the longest x1 5.29 us: per_device(): lax.all_to_all(outgoing, ('gx', 'gy'), split_axis=0, concat_axis=0, tiled...]
    unnamed x13 -> x10, local copies, waits for them, and re-layouts: 11 us -> 6.59 us
    reshape x5 -> x2, local copies, waits for them, and re-layouts: 2.17 us -> 0.15 us  [per_device(): ids.reshape(rup_group, groups_y, slot_dev).transpose(1, 0, 2)]
    dot_general x2 -> x1, matrix products: 2.04 us -> 2.45 us  [per_device(): jnp.einsum('grsv,grsf->rvf', own, slot_spectra, preferred_element_type=jn...]
  transfers between devices with their start and end apart: 2 -> 0, of which waited for: 1 -> 0; matrix products, arithmetic and copies ran while one was open for 10% -> 0% of each run, Pallas kernels for 46% -> 0%
where the time goes in v1:
time: 59.5 us; the launch traced here: 59.3 us
  Pallas kernels  48.3 us (81%)
  local copies, waits for them, and re-layouts  7.44 us (13%)
  matrix products  2.45 us (4%)
  between operations  0.7 us (1%)
    pallas_call x1, Pallas kernels, advance(): pl.pallas_call(functools.partial(step_kernel, dims), out_shape=[jax.Shape...  48.3 us
    unnamed x10, local copies, waits for them, and re-layouts  6.59 us
    dot_general x1, matrix products, per_device(): jnp.einsum('grsv,grsf->rvf', own, slot_spectra, preferred_element_type=jn...  2.45 us

profile of v1, /device:TPU:0, one launch (start us, length us, event | category | flops | bytes accessed | tf_op | source)
XLA Modules:
  0.0 59.3 jit_solution(16815564081874664125)
XLA Ops:
  0.6 48.3 %shard_map.155 = (f32[3,64,32,128]{3,2,1,0:T(8,128)}, f32[64,32,128]{2,1,0:T(8,128)}, f32[64,32,128]{2,1,0:T(8,128)}, f32[64,256]{1,0:T(8,128)}, bf16[8,8,8,128]...) custom-call(f32[3,64,32,128]{3,2,1,0:T(8,128)} %refs_0_.1, f32[64,32,128]{2,1,0:T(8,128)} %refs_1_.1, f32[64,32,128]{2,1,0:T(8,128)} %refs_2_.1, ...), custom_call_target="tpu_custom_call" | custom-call | tf_op jit(solution)/shard_map/pallas_call | solution.py:471
  48.9 0.7 %constant_dynamic-slice_fusion = s32[8,64]{1,0:T(8,128)S(1)} fusion(s32[32,64]{1,0:T(8,128)} %refs_11_.1, s32[]{:T(128)S(6)} %select_n.56), kind=kLoop, calls=%fused_computation.33 | loop fusion | bytes 4100 | tf_op jit(solution)/shard_map/dynamic_slice | solution.py:555
  49.6 0.1 reshape.142
  49.7 0.1 reshape.143
  49.8 0.4 convert_reduce_fusion
  50.2 2.5 %convolution_bitcast_fusion = f32[8,64,256]{2,1,0:T(8,128)} fusion(s32[8,64]{1,0:T(8,128)S(1)} %fusion.13, bf16[512,256]{1,0:T(8,128)(2,1)} %get-tuple-element.16, bf16[8,8,8,128]{3,2,1,0:T(8,128)(2,1)} %get-tuple-element.15, s32[]{:T(128)S(6)} %select_n.55), kind=kOutput, calls=%fused_computation | convolution fusion | flops 151388160 | bytes 919556 | tf_op jit(solution)/shard_map/grsv,grsf->rvf/dot_general | solution.py:571
  52.7 0.0 copy-start.1
  52.7 0.0 copy-start
  52.7 4.0 %copy.27 = f32[3,64,32,128]{3,2,1,0:T(8,128)} copy(f32[3,64,32,128]{3,2,1,0:T(8,128)} %get-tuple-element.22) | data formatting | bytes 6291456
  56.7 0.0 copy-done.1
  56.7 0.0 copy-start.2
  56.7 1.0 %copy.28 = f32[64,32,128]{2,1,0:T(8,128)} copy(f32[64,32,128]{2,1,0:T(8,128)S(1)} %copy-done.1) | data formatting | bytes 2097152
  57.7 0.0 copy-done
  57.7 1.0 %copy.29 = f32[64,32,128]{2,1,0:T(8,128)} copy(f32[64,32,128]{2,1,0:T(8,128)S(1)} %copy-done) | data formatting | bytes 2097152
  58.6 0.0 copy-done.2
  58.6 0.6 %copy.30 = f32[64,256]{1,0:T(8,128)} copy(f32[64,256]{1,0:T(8,128)S(1)} %copy-done.2) | data formatting | bytes 131072
  (4 shorter events, 0.0 us)
Async XLA Ops:
  52.7 4.0 %copy-start.1 = (f32[64,32,128]{2,1,0:T(8,128)S(1)}, f32[64,32,128]{2,1,0:T(8,128)}, u32[]{:S(2)}) copy-start(f32[64,32,128]{2,1,0:T(8,128)} %get-tuple-element.23) | copy-start | bytes 3145732
  52.7 5.0 %copy-start = (f32[64,32,128]{2,1,0:T(8,128)S(1)}, f32[64,32,128]{2,1,0:T(8,128)}, u32[]{:S(2)}) copy-start(f32[64,32,128]{2,1,0:T(8,128)} %get-tuple-element.24) | copy-start | bytes 3145732
  56.7 1.9 %copy-start.2 = (f32[64,256]{1,0:T(8,128)S(1)}, f32[64,256]{1,0:T(8,128)}, u32[]{:S(2)}) copy-start(f32[64,256]{1,0:T(8,128)} %get-tuple-element.25) | copy-start | bytes 196612

commit v2 on v1

--- a/solution.py
+++ b/solution.py
@@ -10,7 +10,7 @@
 
 STEPS = 4
 CAP = 2
-BATCH = 4
+BATCH = 8
 
 
 def phase_rows(freqs):
@@ -21,6 +21,18 @@
 
 Y_ROWS = [4] + [3] * (STEPS - 1) + [1]
 X_PACKS = [3] + [2] * (STEPS - 1) + [1]
+
+
+def quotient(value, size):
+    if size & (size - 1):
+        return lax.div(value, jnp.full_like(value, size))
+    return lax.shift_right_logical(value, jnp.full_like(value, size.bit_length() - 1))
+
+
+def remainder(value, size):
+    if size & (size - 1):
+        return lax.rem(value, jnp.full_like(value, size))
+    return value & (size - 1)
 
 
 def step_kernel(dims, *refs):
@@ -132,7 +144,7 @@
 
     lane = lax.broadcasted_iota(jnp.int32, (ny, nx), 1)
     row = lax.broadcasted_iota(jnp.int32, (ny, nx), 0)
-    quad, lane4 = (lane // 4, lane % 4)
+    quad, lane4 = (quotient(lane, 4), remainder(lane, 4))
     last_lane, first_lane = (lane == nx - 1, lane == 0)
     last_row, first_row = (row == ny - 1, row == 0)
 
@@ -242,10 +254,10 @@
         ruptures, slots = listed.shape
         shape = (per_dev, slots)
         own_ids = lax.broadcasted_iota(jnp.int32, shape, 0) + (gx * ngy + gy) * per_dev
-        slot_owner = lax.broadcasted_iota(jnp.int32, shape, 1) // slot_dev
+        slot_owner = quotient(lax.broadcasted_iota(jnp.int32, shape, 1), slot_dev)
 
         def body(r, best):
-            owner = r // rup_group * ngy + slot_owner
+            owner = quotient(r, rup_group) * ngy + slot_owner
             return jnp.where(listed[pl.ds(r, 1), :] == own_ids, owner, best)
 
         best = lax.fori_loop(0, ruptures, body, jnp.full(shape, -1, jnp.int32))
@@ -341,7 +353,8 @@
 
     fill_placing()
     cells = to_column(cell_row[...].astype(jnp.float32)).astype(jnp.int32)
-    cell_z, cell_y, cell_x = (cells // (ny * nx), (cells // nx) % ny, cells % nx)
+    cell_z, cell_x = (quotient(cells, ny * nx), remainder(cells, nx))
+    cell_y = remainder(quotient(cells, nx), ny)
     patch_lane = lax.broadcasted_iota(jnp.int32, (per_dev, nx), 1)
 
     def masked(keep, values):
@@ -350,7 +363,7 @@
     def sample_own(n):
         def body(i, carry):
             at = cell[i]
-            z, y = (at // (ny * nx), (at // nx) % ny)
+            z, y = (quotient(at, ny * nx), remainder(quotient(at, nx), ny))
             out = pl.ds(i, 1)
             rows_got[0, out, :] = vx[z, pl.ds(jnp.minimum(y + 1, ny - 1), 1), :]
             rows_got[1, out, :] = vx[z, pl.ds(jnp.maximum(y - 1, 0), 1), :]
@@ -369,8 +382,8 @@
 
         def body(i, carry):
             at = cell[i]
-            z, y = (at // (ny * nx), (at // nx) % ny)
-            c, zl = (z // zc, z % zc)
+            z, y = (quotient(at, ny * nx), remainder(quotient(at, nx), ny))
+            c, zl = (quotient(z, zc), remainder(z, zc))
             out = pl.ds(i, 1)
             rows_got[0, out, :] = yrecv[n][0, c, which_row, pl.ds(zl, 1), :]
             rows_got[1, out, :] = yrecv[n][1, c, which_row, pl.ds(zl, 1), :]
@@ -379,7 +392,7 @@
             return carry
 
         lax.fori_loop(0, per_dev, body, 0, unroll=8)
-        start = 4 * (cell_z % zc)
+        start = 4 * remainder(cell_z, zc)
         here = patch_lane == cell_x
         total = samples[n - 1]
         total = total + masked(here & (cell_y == ny - 1), rows_got[1])

time: 59.5 us -> 52 us (0.87)
  Pallas kernels: 48.3 us -> 40.8 us
    pallas_call x1, Pallas kernels: 48.3 us -> 40.8 us  [advance(): pl.pallas_call(functools.partial(step_kernel, dims), out_shape=[jax.Shape...]
where the time goes in v2:
time: 52 us; the launch traced here: 51.8 us
  Pallas kernels  40.8 us (78%)
  local copies, waits for them, and re-layouts  7.44 us (14%)
  matrix products  2.45 us (5%)
  between operations  0.7 us (1%)
    pallas_call x1, Pallas kernels, advance(): pl.pallas_call(functools.partial(step_kernel, dims), out_shape=[jax.Shape...  40.8 us
    unnamed x10, local copies, waits for them, and re-layouts  6.59 us
    dot_general x1, matrix products, per_device(): jnp.einsum('grsv,grsf->rvf', own, slot_spectra, preferred_element_type=jn...  2.45 us

profile of v2, /device:TPU:0, one launch (start us, length us, event | category | flops | bytes accessed | tf_op | source)
XLA Modules:
  0.0 51.8 jit_solution(3348976481855370502)
XLA Ops:
  0.6 40.8 %shard_map.155 = (f32[3,64,32,128]{3,2,1,0:T(8,128)}, f32[64,32,128]{2,1,0:T(8,128)}, f32[64,32,128]{2,1,0:T(8,128)}, f32[64,256]{1,0:T(8,128)}, bf16[8,8,8,128]...) custom-call(f32[3,64,32,128]{3,2,1,0:T(8,128)} %refs_0_.1, f32[64,32,128]{2,1,0:T(8,128)} %refs_1_.1, f32[64,32,128]{2,1,0:T(8,128)} %refs_2_.1, ...), custom_call_target="tpu_custom_call" | custom-call | tf_op jit(solution)/shard_map/pallas_call | solution.py:484
  41.4 0.7 %constant_dynamic-slice_fusion = s32[8,64]{1,0:T(8,128)S(1)} fusion(s32[32,64]{1,0:T(8,128)} %refs_11_.1, s32[]{:T(128)S(6)} %select_n.56), kind=kLoop, calls=%fused_computation.33 | loop fusion | bytes 4100 | tf_op jit(solution)/shard_map/dynamic_slice | solution.py:568
  42.1 0.1 reshape.142
  42.2 0.1 reshape.143
  42.3 0.4 convert_reduce_fusion
  42.7 2.5 %convolution_bitcast_fusion = f32[8,64,256]{2,1,0:T(8,128)} fusion(s32[8,64]{1,0:T(8,128)S(1)} %fusion.13, bf16[512,256]{1,0:T(8,128)(2,1)} %get-tuple-element.16, bf16[8,8,8,128]{3,2,1,0:T(8,128)(2,1)} %get-tuple-element.15, s32[]{:T(128)S(6)} %select_n.55), kind=kOutput, calls=%fused_computation | convolution fusion | flops 151388160 | bytes 919556 | tf_op jit(solution)/shard_map/grsv,grsf->rvf/dot_general | solution.py:584
  45.2 0.0 copy-start.1
  45.2 0.0 copy-start
  45.2 4.0 %copy.27 = f32[3,64,32,128]{3,2,1,0:T(8,128)} copy(f32[3,64,32,128]{3,2,1,0:T(8,128)} %get-tuple-element.22) | data formatting | bytes 6291456
  49.2 0.0 copy-done.1
  49.2 0.0 copy-start.2
  49.2 1.0 %copy.28 = f32[64,32,128]{2,1,0:T(8,128)} copy(f32[64,32,128]{2,1,0:T(8,128)S(1)} %copy-done.1) | data formatting | bytes 2097152
  50.2 0.0 copy-done
  50.2 1.0 %copy.29 = f32[64,32,128]{2,1,0:T(8,128)} copy(f32[64,32,128]{2,1,0:T(8,128)S(1)} %copy-done) | data formatting | bytes 2097152
  51.1 0.0 copy-done.2
  51.1 0.6 %copy.30 = f32[64,256]{1,0:T(8,128)} copy(f32[64,256]{1,0:T(8,128)S(1)} %copy-done.2) | data formatting | bytes 131072
  (4 shorter events, 0.0 us)
Async XLA Ops:
  45.2 4.0 %copy-start.1 = (f32[64,32,128]{2,1,0:T(8,128)S(1)}, f32[64,32,128]{2,1,0:T(8,128)}, u32[]{:S(2)}) copy-start(f32[64,32,128]{2,1,0:T(8,128)} %get-tuple-element.23) | copy-start | bytes 3145732
  45.2 5.0 %copy-start = (f32[64,32,128]{2,1,0:T(8,128)S(1)}, f32[64,32,128]{2,1,0:T(8,128)}, u32[]{:S(2)}) copy-start(f32[64,32,128]{2,1,0:T(8,128)} %get-tuple-element.24) | copy-start | bytes 3145732
  49.2 1.9 %copy-start.2 = (f32[64,256]{1,0:T(8,128)S(1)}, f32[64,256]{1,0:T(8,128)}, u32[]{:S(2)}) copy-start(f32[64,256]{1,0:T(8,128)} %get-tuple-element.25) | copy-start | bytes 196612
